TPU v7x, 512 devices: a whole 4x4x16 slice. The times are simulated.
512 devices in a mesh: rows: 128 (over x, z, core), rep: 4 (over y).
Axes of the slice: x: 4, y: 4, z: 16, core: 2. Of those that a mesh axis runs over, the one named last changes fastest.
Arguments:
- feats: bfloat16 [4, 32768, 512], P('rep', 'rows'), may hold values from -24 to 24
- grad_out: bfloat16 [4, 32768, 512], P('rep', 'rows'), may hold values from -6 to 6
- qkv_weight: bfloat16 [512, 1536], P('rows'), may hold values from -0.25 to 0.25
- proj_weight: bfloat16 [512, 512], P('rows'), may hold values from -0.25 to 0.25
- to_hilbert: int32 [4, 16384], P('rep', 'rows'), may hold values from 0 to 16383, as said below
- to_zorder: int32 [4, 16384], P('rep', 'rows'), may hold values from 0 to 16383, as said below
Outputs:
- grad_feats: bfloat16 [4, 32768, 512], P('rep', 'rows')
- qkv_grad: float32 [512, 1536], P('rows')
- proj_grad: float32 [512, 512], P('rows')
Inputs may be any that keep to these rules, and one draw needn't show every extreme that they name: to_hilbert[s] is a permutation of the blocks of scene s and to_zorder[s] its inverse; of the 128 Z-order blocks of one device, at most 2 have Hilbert positions on any one device, and exactly 2 for some pair of devices in every scene. `to_zorder`: the inverse of to_hilbert in every scene.
All inputs are finite; a program needn't handle non-finite values.
Results may differ from a plain program's by a relative error of at most 0.015.
The roundings to bfloat16 on the way count: a program that leaves them out, or rounds other values in their place, can miss the bound.
Values may be sent and summed in bfloat16 or wider, within the bound.
No kernel may reach another device: no remote copies, remote signals or barrier semaphores. Data moves between devices by JAX's collectives and lax.ppermute only.
A program may use at most 64 MiB of HBM per device.

v0:
```python
import jax
import jax.numpy as jnp
from jax import lax
from jax.sharding import PartitionSpec as P

HEADS = 8
CAP = 2


def from_partner(block, axis, apart):
    count = lax.axis_size(axis)
    route = []
    for low in range(count):
        high = low | 1 << apart
        if high != low and high < count:
            route += [(low, high), (high, low)]
    return lax.ppermute(block, axis, route)


def move_blocks(outgoing):
    return lax.all_to_all(outgoing, "rows", split_axis=0, concat_axis=0, tiled=True)


def rank_within(order_keys, owners):
    same_owner = owners[None, :] == owners[:, None]
    earlier = order_keys[None, :] < order_keys[:, None]
    return jnp.sum(jnp.logical_and(same_owner, earlier).astype(jnp.int32), axis=1)


def contract_rows(left, right):
    return lax.dot_general(
        left, right, (((0,), (0,)), ((), ())), preferred_element_type=jnp.float32
    )


def contract_cols(left, right):
    return lax.dot_general(
        left, right, (((1,), (1,)), ((), ())), preferred_element_type=jnp.float32
    )


def per_device(feats, grad_out, qkv_weight, proj_weight, to_hilbert, to_zorder):
    peer_count = lax.axis_size("rows")
    feature = feats[0]
    rows_dev, channels = feature.shape
    head_size = channels // HEADS
    scale = head_size ** (-0.5)
    blocks_dev = to_hilbert.shape[1]
    slot_count = peer_count * CAP
    w_qkv, w_proj = (
        lax.all_gather(qkv_weight, "rows", axis=0, tiled=True),
        lax.all_gather(proj_weight, "rows", axis=0, tiled=True),
    )
    forward_list = to_hilbert[0]
    inverse_list = to_zorder[0]
    local_ids = jnp.arange(blocks_dev, dtype=jnp.int32)
    slot_ids = jnp.arange(slot_count, dtype=jnp.int32)
    target_dev = forward_list // blocks_dev
    send_slot = target_dev * CAP + rank_within(local_ids, target_dev)
    send_table = (send_slot[None, :] == slot_ids[:, None]).astype(jnp.bfloat16)
    source_dev = inverse_list // blocks_dev
    recv_slot = source_dev * CAP + rank_within(inverse_list, source_dev)
    recv_table = (recv_slot[:, None] == slot_ids[None, :]).astype(jnp.bfloat16)
    zblocks = grad_out[0].reshape(blocks_dev, -1)
    outgoing = jnp.dot(send_table, zblocks, preferred_element_type=jnp.float32).astype(jnp.bfloat16)
    arrived = move_blocks(outgoing.reshape(peer_count, CAP, -1)).reshape(slot_count, -1)
    grad_hil = jnp.dot(recv_table, arrived, preferred_element_type=jnp.float32).astype(jnp.bfloat16)
    grad_hil = grad_hil.reshape(rows_dev, channels)
    qkv = jnp.dot(feature, w_qkv, preferred_element_type=jnp.float32).astype(jnp.bfloat16)
    query = qkv[:, :channels]
    keyval = qkv[:, channels:]
    grad_attn = contract_cols(grad_hil, w_proj).astype(jnp.bfloat16)
    other_kv = from_partner(keyval, "rows", 0)
    keys_all = jnp.concatenate([keyval[:, :channels], other_kv[:, :channels]], axis=0)
    values_all = jnp.concatenate([keyval[:, channels:], other_kv[:, channels:]], axis=0)
    attn_parts, dq_parts, dk_parts, dv_parts = ([], [], [], [])
    for head_index in range(HEADS):
        lo_col = head_index * head_size
        q_head = query[:, lo_col : lo_col + head_size]
        k_head = keys_all[:, lo_col : lo_col + head_size]
        v_head = values_all[:, lo_col : lo_col + head_size]
        g_head = grad_attn[:, lo_col : lo_col + head_size]
        score = contract_cols(q_head, k_head) * scale
        row_max = jnp.max(score, axis=1, keepdims=True)
        raised = jnp.exp(score - row_max)
        row_sum = jnp.sum(raised, axis=1, keepdims=True)
        probs = raised / row_sum
        probs_b = probs.astype(jnp.bfloat16)
        attn_parts.append(
            jnp.dot(probs_b, v_head, preferred_element_type=jnp.float32).astype(jnp.bfloat16)
        )
        dprob = contract_cols(g_head, v_head)
        delta = jnp.sum(probs * dprob, axis=1, keepdims=True)
        dscore = (probs * (dprob - delta) * scale).astype(jnp.bfloat16)
        dq_parts.append(jnp.dot(dscore, k_head, preferred_element_type=jnp.float32))
        dk_parts.append(contract_rows(dscore, q_head))
        dv_parts.append(contract_rows(probs_b, g_head))
    grad_q = jnp.concatenate(dq_parts, axis=1)
    grad_k = jnp.concatenate(dk_parts, axis=1)
    grad_v = jnp.concatenate(dv_parts, axis=1)
    other_k, other_v = (
        from_partner(grad_k[rows_dev:].astype(jnp.bfloat16), "rows", 0).astype(jnp.float32),
        from_partner(grad_v[rows_dev:].astype(jnp.bfloat16), "rows", 0).astype(jnp.float32),
    )
    grad_k = grad_k[:rows_dev] + other_k
    grad_v = grad_v[:rows_dev] + other_v
    grad_qkv = jnp.concatenate([grad_q, grad_k, grad_v], axis=1).astype(jnp.bfloat16)
    attn = jnp.concatenate(attn_parts, axis=1)
    grad_hfeat = contract_cols(grad_qkv, w_qkv).astype(jnp.bfloat16)
    hblocks = grad_hfeat.reshape(blocks_dev, -1)
    going_back = contract_rows(recv_table, hblocks).astype(jnp.bfloat16)
    returned = move_blocks(going_back.reshape(peer_count, CAP, -1)).reshape(slot_count, -1)
    grad_z = contract_rows(send_table, returned).astype(jnp.bfloat16).reshape(rows_dev, channels)
    share = channels // peer_count
    term = jnp.concatenate(
        [contract_rows(feature, grad_qkv), contract_rows(attn, grad_hil)], axis=1
    )
    total = lax.psum(term, ("rows", "rep"))
    owned = lax.dynamic_slice_in_dim(total, lax.axis_index("rows") * share, share, 0)
    return (grad_z[None], owned[:, : 3 * channels], owned[:, 3 * channels :])


def solution(mesh):
    placed = (
        P("rep", "rows", None),
        P("rep", "rows", None),
        P("rows", None),
        P("rows", None),
        P("rep", "rows"),
        P("rep", "rows"),
    )
    return jax.shard_map(
        per_device,
        mesh=mesh,
        in_specs=placed,
        out_specs=(P("rep", "rows", None), P("rows", None), P("rows", None)),
        check_vma=False,
    )
```

profile of v0, /device:TPU:2, one launch (start us, length us, event | category | flops | bytes accessed | tf_op | source)
XLA Modules:
  0.0 721.0 jit_solution(14029525855574183305)
XLA Ops:
  7.2 0.7 all-gather.4.cloned.1.call-update
  7.9 1.0 reshape_squeeze.3
  9.0 0.7 and_select_fusion.2
  9.6 0.7 fusion.202
  10.5 0.7 fusion.113
  11.5 1.0 reshape.119
  12.5 19.5 %all-to-all-start = ((bf16[128,2,1024]{2,1,0:T(2,128)(2,1)}), bf16[128,2,1024]{2,1,0:T(2,128)(2,1)S(1)}, u32[]{:S(2)}, u32[]{:S(2)}) async-start(bf16[128,2,1024]{2,1,0:T(2,128)(2,1)} %reshape.119), calls=%async_computation | async-start | bytes 1048576 | tf_op jit(solution)/shard_map/all_to_all | solution.py:21
  32.0 100.5 %all-gather.1 = bf16[128,4,512]{2,1,0:T(4,128)(2,1)S(1)} all-gather(bf16[1,4,512]{2,1,0:T(4,128)(2,1)S(1)} %bitcast.64), channel_id=1, replica_groups=mesh['rows'=128,'rep'=4] {'rows'}, dimensions={0}, use_global_device_ids=true | all-gather | bytes 528384 | tf_op jit(solution)/shard_map/all_gather | solution.py:52
  132.9 1.0 reshape.120
  133.9 22.9 %all-gather.4.cloned.1.call-done = bf16[128,4,1536]{2,1,0:T(4,128)(2,1)} async-done(((bf16[1,4,1536]{2,1,0:T(4,128)(2,1)}), bf16[128,4,1536]{2,1,0:T(4,128)(2,1)}) %all-gather.4.cloned.1.call-update) | async-done | bytes 1572880 | tf_op jit(solution)/shard_map/all_gather | solution.py:51
  156.9 2.7 reshape.126
  159.6 0.6 convolution_convert_fusion
  160.2 0.9 slice.187
  161.0 2.3 collective-permute-start
  163.4 1.0 convolution_convert_fusion.6
  164.4 1.0 reshape.121
  165.8 1.1 fusion.160
  168.6 0.4 fusion.162
  169.3 0.4 fusion.164
  170.0 0.4 fusion.166
  171.4 0.4 fusion.168
  172.0 0.4 multiply_reduce_fusion.6
  172.7 0.4 fusion.6
  174.5 0.4 multiply_reduce_fusion.4
  175.2 0.4 fusion.4
  175.8 0.3 multiply_reduce_fusion.3
  176.9 0.4 multiply_reduce_fusion.2
  177.7 0.4 fusion.2
  179.1 0.4 multiply_reduce_fusion
  180.5 2.1 collective-permute-start.2
  182.6 1.3 fusion.169
  188.6 2.4 collective-permute-start.1
  191.4 0.6 collective-permute-done.1
  192.2 1.3 convolution_convert_fusion.4
  193.6 0.6 convolution_bitcast_fusion
  194.1 1.7 reshape.122
  195.8 2.2 convolution_convert_fusion.1
  198.0 2.1 reshape.123
  200.1 12.8 %all-to-all-start.1 = ((bf16[128,2,1024]{2,1,0:T(2,128)(2,1)}), bf16[128,2,1024]{2,1,0:T(2,128)(2,1)}, u32[]{:S(2)}, u32[]{:S(2)}) async-start(bf16[128,2,1024]{2,1,0:T(2,128)(2,1)} %reshape.123), calls=%async_computation.1 | async-start | bytes 1048576 | tf_op jit(solution)/shard_map/all_to_all | solution.py:21
  212.9 3.6 pad_maximum_fusion
  216.5 29.6 %all-to-all-done.1 = bf16[128,2,1024]{2,1,0:T(2,128)(2,1)} async-done(((bf16[128,2,1024]{2,1,0:T(2,128)(2,1)}), bf16[128,2,1024]{2,1,0:T(2,128)(2,1)}, u32[]{:S(2)}, u32[]{:S(2)}) %all-to-all-start.1) | async-done | bytes 524320 | tf_op jit(solution)/shard_map/all_to_all | solution.py:21
  246.2 1.2 reshape.124
  247.7 0.8 broadcast_in_dim_reshape.3
  248.5 461.6 %all-reduce.2.cloned.1.call-done = f32[512,2048]{0,1:T(8,128)} async-done(((f32[512,2048]{0,1:T(8,128)}), f32[512,2048]{0,1:T(8,128)}) %all-reduce.2.cloned.1.call-update) | async-done | bytes 4194320 | tf_op jit(solution)/shard_map/psum | solution.py:118
  710.0 1.4 constant_dynamic-slice_fusion
  711.4 0.9 copy.13
  712.3 1.1 dynamic-slice.1
  713.4 0.7 copy.14
  (82 shorter events, 15.7 us)
Async XLA Ops:
  7.2 152.4 %copy-start = (bf16[1,256,512]{2,1,0:T(8,128)(2,1)S(1)}, bf16[1,256,512]{2,1,0:T(8,128)(2,1)}, u32[]{:S(2)}) copy-start(bf16[1,256,512]{2,1,0:T(8,128)(2,1)} %param.6) | copy-start | bytes 786436
  7.2 24.8 %copy-start.2 = (bf16[4,512]{1,0:T(4,128)(2,1)S(1)}, bf16[4,512]{1,0:T(4,128)(2,1)}, u32[]{:S(2)}) copy-start(bf16[4,512]{1,0:T(4,128)(2,1)} %param.9) | copy-start | bytes 12292
  7.2 125.5 %copy-start.3 = (s32[1,128]{1,0:T(1,128)S(1)}, s32[1,128]{1,0:T(1,128)}, u32[]{:S(2)}) copy-start(s32[1,128]{1,0:T(1,128)} %param.11) | copy-start | bytes 1540
  7.2 149.7 %all-gather.4.cloned.1.call-start = ((), (), s32[]{:S(2)}) async-start(), calls=%async_computation.3 | async-start | bytes 1585152 | tf_op jit(solution)/shard_map/all_gather | solution.py:51
  12.5 120.5 %all-to-all-start = ((bf16[128,2,1024]{2,1,0:T(2,128)(2,1)}), bf16[128,2,1024]{2,1,0:T(2,128)(2,1)S(1)}, u32[]{:S(2)}, u32[]{:S(2)}) async-start(bf16[128,2,1024]{2,1,0:T(2,128)(2,1)} %reshape.119), calls=%async_computation | async-start | bytes 1048576 | tf_op jit(solution)/shard_map/all_to_all | solution.py:21
  159.6 3.8 copy-start.1
  161.0 4.8 collective-permute-start
  180.5 11.7 %collective-permute-start.2 = (bf16[256,512]{0,1:T(8,128)(2,1)S(1)}, bf16[256,512]{0,1:T(8,128)(2,1)S(1)}, u32[]{:S(2)}, u32[]{:S(2)}) collective-permute-start(bf16[256,512]{0,1:T(8,128)(2,1)S(1)} %slice.454), channel_id=1, source_target_pairs={{0,4},{4,0},{8,12},{12,8},{16,20},{20,16},{24,28},{28,24},{32,36},... | collective-permute-start | bytes 786440 | tf_op jit(solution)/shard_map/ppermute | solution.py:17
  188.6 3.4 collective-permute-start.1
  200.1 46.1 %all-to-all-start.1 = ((bf16[128,2,1024]{2,1,0:T(2,128)(2,1)}), bf16[128,2,1024]{2,1,0:T(2,128)(2,1)}, u32[]{:S(2)}, u32[]{:S(2)}) async-start(bf16[128,2,1024]{2,1,0:T(2,128)(2,1)} %reshape.123), calls=%async_computation.1 | async-start | bytes 1048576 | tf_op jit(solution)/shard_map/all_to_all | solution.py:21
  212.9 497.2 %all-reduce.2.cloned.1.call-start = ((), (), s32[]{:S(2)}) async-start(), calls=%async_computation.2 | async-start | bytes 8388608 | tf_op jit(solution)/shard_map/psum | solution.py:118
Sparse Core Ops, SparseCore 0:
  11.1 145.7 all-gather.3
  219.2 490.8 all-reduce.1
where the time goes:
time: 722 us; the launch traced here: 721 us
  waiting for transfers between devices  515 us (71%)
  blocking collectives  101 us (14%)
  starting transfers between devices  39.3 us (5%)
  matrix products  22.5 us (3%)
  local copies, waits for them, and re-layouts  18.9 us (3%)
  between operations  14.4 us (2%)
  other arithmetic  9.94 us (1%)
    psum x1, waiting for transfers between devices, per_device(): total = lax.psum(term, ('rows', 'rep'))  462 us
    all_gather x1, blocking collectives, per_device(): lax.all_gather(proj_weight, 'rows', axis=0, tiled=True)  101 us
    all_to_all x2, starting transfers between devices, move_blocks(): lax.all_to_all(outgoing, 'rows', split_axis=0, concat_axis=0, tiled=True)  32.3 us
    all_to_all x2, waiting for transfers between devices, move_blocks(): lax.all_to_all(outgoing, 'rows', split_axis=0, concat_axis=0, tiled=True)  29.6 us
    all_gather x1, waiting for transfers between devices, per_device(): lax.all_gather(qkv_weight, 'rows', axis=0, tiled=True)  22.9 us
  transfers between devices with their start and end apart: 7, of which 4 were waited for; matrix products, arithmetic and copies ran while one was open for 3% of the time, Pallas kernels for 0%

commit v1 on v0

--- a/solution.py
+++ b/solution.py
@@ -115,7 +115,7 @@
     term = jnp.concatenate(
         [contract_rows(feature, grad_qkv), contract_rows(attn, grad_hil)], axis=1
     )
-    total = lax.psum(term, ("rows", "rep"))
+    total = lax.psum(lax.psum(term, "rows"), "rep")
     owned = lax.dynamic_slice_in_dim(total, lax.axis_index("rows") * share, share, 0)
     return (grad_z[None], owned[:, : 3 * channels], owned[:, 3 * channels :])
 

time: 722 us -> 672 us (0.931)
  the two profiles are of different devices: /device:TPU:2 before, /device:TPU:1 now
where the time goes in v1:
time: 672 us; the launch traced here: 671 us
  waiting for transfers between devices  470 us (70%)
  blocking collectives  101 us (15%)
  starting transfers between devices  42.4 us (6%)
  matrix products  19 us (3%)
  local copies, waits for them, and re-layouts  16.1 us (2%)
  between operations  14.2 us (2%)
  other arithmetic  8.76 us (1%)
    psum x2, waiting for transfers between devices, per_device(): total = lax.psum(lax.psum(term, 'rows'), 'rep')  411 us
    all_gather x1, blocking collectives, per_device(): lax.all_gather(proj_weight, 'rows', axis=0, tiled=True)  101 us
    all_to_all x2, starting transfers between devices, move_blocks(): lax.all_to_all(outgoing, 'rows', split_axis=0, concat_axis=0, tiled=True)  35.4 us
    all_to_all x2, waiting for transfers between devices, move_blocks(): lax.all_to_all(outgoing, 'rows', split_axis=0, concat_axis=0, tiled=True)  33.2 us
    all_gather x1, waiting for transfers between devices, per_device(): lax.all_gather(qkv_weight, 'rows', axis=0, tiled=True)  23.7 us
  transfers between devices with their start and end apart: 8, of which 5 were waited for; matrix products, arithmetic and copies ran while one was open for 3% of the time, Pallas kernels for 0%

profile of v1, /device:TPU:1, one launch (start us, length us, event | category | flops | bytes accessed | tf_op | source)
XLA Modules:
  0.0 671.2 jit_solution(14868801363304208827)
XLA Ops:
  7.2 0.7 all-gather.4.cloned.1.call-update
  7.9 1.0 reshape_squeeze.3
  9.0 0.7 and_select_fusion.2
  9.6 0.7 fusion.202
  10.5 0.7 fusion.113
  11.5 1.0 reshape.119
  12.5 20.4 %all-to-all-start = ((bf16[128,2,1024]{2,1,0:T(2,128)(2,1)}), bf16[128,2,1024]{2,1,0:T(2,128)(2,1)S(1)}, u32[]{:S(2)}, u32[]{:S(2)}) async-start(bf16[128,2,1024]{2,1,0:T(2,128)(2,1)} %reshape.119), calls=%async_computation | async-start | bytes 1048576 | tf_op jit(solution)/shard_map/all_to_all | solution.py:21
  32.9 101.0 %all-gather.1 = bf16[128,4,512]{2,1,0:T(4,128)(2,1)S(1)} all-gather(bf16[1,4,512]{2,1,0:T(4,128)(2,1)S(1)} %bitcast.64), channel_id=1, replica_groups=mesh['rows'=128,'rep'=4] {'rows'}, dimensions={0}, use_global_device_ids=true | all-gather | bytes 528384 | tf_op jit(solution)/shard_map/all_gather | solution.py:52
  134.4 1.0 reshape.120
  135.4 23.7 %all-gather.4.cloned.1.call-done = bf16[128,4,1536]{2,1,0:T(4,128)(2,1)} async-done(((bf16[1,4,1536]{2,1,0:T(4,128)(2,1)}), bf16[128,4,1536]{2,1,0:T(4,128)(2,1)}) %all-gather.4.cloned.1.call-update) | async-done | bytes 1572880 | tf_op jit(solution)/shard_map/all_gather | solution.py:51
  159.1 2.7 reshape.126
  161.9 0.6 convolution_convert_fusion
  162.5 0.9 slice.187
  163.3 2.3 collective-permute-start
  165.7 1.0 convolution_convert_fusion.6
  166.6 1.0 reshape.121
  168.1 1.1 fusion.160
  170.8 0.4 fusion.162
  171.5 0.4 fusion.164
  172.3 0.4 fusion.166
  173.6 0.4 fusion.168
  174.2 0.4 multiply_reduce_fusion.6
  174.9 0.4 fusion.6
  176.7 0.4 multiply_reduce_fusion.4
  177.4 0.4 fusion.4
  178.0 0.3 multiply_reduce_fusion.3
  179.2 0.4 multiply_reduce_fusion.2
  179.9 0.4 fusion.2
  181.4 0.4 multiply_reduce_fusion
  182.7 2.2 collective-permute-start.2
  184.9 0.3 fusion.169
  189.9 2.4 collective-permute-start.1
  192.7 0.6 collective-permute-done.1
  193.5 0.9 copy-done.2
  194.5 0.6 convolution_bitcast_fusion
  195.0 2.4 pad_maximum_fusion
  197.5 352.6 %all-reduce.3.cloned.1.call-done = f32[512,2048]{0,1:T(8,128)} async-done(((f32[512,2048]{0,1:T(8,128)}), f32[512,2048]{0,1:T(8,128)}) %all-reduce.3.cloned.1.call-update) | async-done | bytes 4194320 | tf_op jit(solution)/shard_map/psum | solution.py:118
  550.1 0.6 convolution_convert_fusion.4
  550.8 0.4 convolution_convert_fusion.1
  551.3 1.0 reshape.123
  552.3 15.0 %all-to-all-start.1 = ((bf16[128,2,1024]{2,1,0:T(2,128)(2,1)}), bf16[128,2,1024]{2,1,0:T(2,128)(2,1)S(1)}, u32[]{:S(2)}, u32[]{:S(2)}) async-start(bf16[128,2,1024]{2,1,0:T(2,128)(2,1)} %reshape.123), calls=%async_computation.1 | async-start | bytes 1048576 | tf_op jit(solution)/shard_map/all_to_all | solution.py:21
  567.3 33.2 %all-to-all-done.1 = bf16[128,2,1024]{2,1,0:T(2,128)(2,1)S(1)} async-done(((bf16[128,2,1024]{2,1,0:T(2,128)(2,1)}), bf16[128,2,1024]{2,1,0:T(2,128)(2,1)S(1)}, u32[]{:S(2)}, u32[]{:S(2)}) %all-to-all-start.1) | async-done | bytes 524320 | tf_op jit(solution)/shard_map/all_to_all | solution.py:21
  601.0 0.8 broadcast_in_dim_reshape.3
  601.8 58.8 %all-reduce.5.cloned.1.call-done = f32[512,2048]{0,1:T(8,128)} async-done(((f32[512,2048]{0,1:T(8,128)}), f32[512,2048]{0,1:T(8,128)}) %all-reduce.5.cloned.1.call-update) | async-done | bytes 4194320 | tf_op jit(solution)/shard_map/psum | solution.py:118
  660.6 1.4 constant_dynamic-slice_fusion
  662.0 0.9 copy.13
  662.8 1.1 dynamic-slice.1
  663.9 0.7 copy.14
  (89 shorter events, 16.0 us)
Async XLA Ops:
  7.2 154.7 %copy-start = (bf16[1,256,512]{2,1,0:T(8,128)(2,1)S(1)}, bf16[1,256,512]{2,1,0:T(8,128)(2,1)}, u32[]{:S(2)}) copy-start(bf16[1,256,512]{2,1,0:T(8,128)(2,1)} %param.6) | copy-start | bytes 786436
  7.2 25.7 %copy-start.4 = (bf16[4,512]{1,0:T(4,128)(2,1)S(1)}, bf16[4,512]{1,0:T(4,128)(2,1)}, u32[]{:S(2)}) copy-start(bf16[4,512]{1,0:T(4,128)(2,1)} %param.9) | copy-start | bytes 12292
  7.2 126.9 %copy-start.5 = (s32[1,128]{1,0:T(1,128)S(1)}, s32[1,128]{1,0:T(1,128)}, u32[]{:S(2)}) copy-start(s32[1,128]{1,0:T(1,128)} %param.11) | copy-start | bytes 1540
  7.2 151.9 %all-gather.4.cloned.1.call-start = ((), (), s32[]{:S(2)}) async-start(), calls=%async_computation.4 | async-start | bytes 1585152 | tf_op jit(solution)/shard_map/all_gather | solution.py:51
  12.5 121.9 %all-to-all-start = ((bf16[128,2,1024]{2,1,0:T(2,128)(2,1)}), bf16[128,2,1024]{2,1,0:T(2,128)(2,1)S(1)}, u32[]{:S(2)}, u32[]{:S(2)}) async-start(bf16[128,2,1024]{2,1,0:T(2,128)(2,1)} %reshape.119), calls=%async_computation | async-start | bytes 1048576 | tf_op jit(solution)/shard_map/all_to_all | solution.py:21
  32.9 517.2 %all-reduce.3.cloned.1.call-start = ((), (), s32[]{:S(2)}) async-start(), calls=%async_computation.2 | async-start | bytes 8388608 | tf_op jit(solution)/shard_map/psum | solution.py:118
  161.9 3.8 copy-start.1
  163.3 4.7 collective-permute-start
  182.7 10.7 %collective-permute-start.2 = (bf16[256,512]{0,1:T(8,128)(2,1)S(1)}, bf16[256,512]{0,1:T(8,128)(2,1)S(1)}, u32[]{:S(2)}, u32[]{:S(2)}) collective-permute-start(bf16[256,512]{0,1:T(8,128)(2,1)S(1)} %slice.454), channel_id=1, source_target_pairs={{0,4},{4,0},{8,12},{12,8},{16,20},{20,16},{24,28},{28,24},{32,36},... | collective-permute-start | bytes 786440 | tf_op jit(solution)/shard_map/ppermute | solution.py:17
  189.9 3.4 collective-permute-start.1
  193.5 0.9 copy-start.2
  197.5 352.6 %copy-start.3 = (bf16[256,1536]{0,1:T(8,128)(2,1)S(1)}, bf16[256,1536]{0,1:T(8,128)(2,1)}, u32[]{:S(2)}) copy-start(bf16[256,1536]{0,1:T(8,128)(2,1)} %copy-done.2) | copy-start | bytes 2359300
  197.5 463.1 %all-reduce.5.cloned.1.call-start = ((), (), s32[]{:S(2)}) async-start(), calls=%async_computation.3 | async-start | bytes 8388608 | tf_op jit(solution)/shard_map/psum | solution.py:118
  552.3 48.2 %all-to-all-start.1 = ((bf16[128,2,1024]{2,1,0:T(2,128)(2,1)}), bf16[128,2,1024]{2,1,0:T(2,128)(2,1)S(1)}, u32[]{:S(2)}, u32[]{:S(2)}) async-start(bf16[128,2,1024]{2,1,0:T(2,128)(2,1)} %reshape.123), calls=%async_computation.1 | async-start | bytes 1048576 | tf_op jit(solution)/shard_map/all_to_all | solution.py:21
Sparse Core Ops, SparseCore 0:
  11.1 147.9 all-gather.3
  197.6 352.4 all-reduce.2
  552.6 107.9 all-reduce.4
